TPU v7x, 32 devices: a whole 2x2x4 slice. The times are simulated.
32 devices in a mesh: row: 8 (over y, x, core), col: 4 (over z).
Axes of the slice: x: 2, y: 2, z: 4, core: 2. Of those that a mesh axis runs over, the one named last changes fastest.
Arguments:
- x_mat: float32 [512, 512], replicated, may hold values from -8 to 40, as said below
- y_inv: float32 [512, 512], replicated, may hold values from -8 to 40, as said below
- panel_blocks: bfloat16 [512, 4096], replicated, may hold values from -6 to 6
- panel_pos: int32 [512], replicated, may hold values from 0 to 63
- group_blocks: int32 [32, 2], replicated, may hold values from 0 to 63
- cons_blocks: bfloat16 [57344, 4096], P(('row', 'col')), may hold values from -6 to 6
- slot_block: int32 [57344], P(('row', 'col')), may hold values from 0 to 1
- slot_row: int32 [57344], P(('row', 'col')), may hold values from 0 to 32767, as said below
- group_size: int32 [32], P(('row', 'col')), may hold values from 768 to 1792, as said below
- trailing: float32 [32768, 2048], P('row', 'col'), may hold values from -6 to 6
Outputs:
- lower_panel: float32 [32768, 512], P(('row', 'col'))
- updated: float32 [32768, 2048], P('row', 'col')
Inputs may be any that keep to these rules, and one draw needn't show every extreme that they name: `x_mat`: symmetric positive definite. `y_inv`: symmetric positive definite. `slot_row`: over all groups, the live slots hold every row 0 to 32767 exactly once; the live slots of one group hold at most 56 rows of one aligned range of 1024 rows, and that most is reached in every draw; other slots hold arbitrary rows. `group_size`: the live slots of a group are its first slots; some group has exactly 1792 in every draw.
All inputs are finite; a program needn't handle non-finite values.
Results may differ from a plain program's by a relative error of at most 0.004.
Values may be sent and summed in bfloat16 or wider, within the bound.
A program may use at most 192 MiB of HBM per device.

v0:
```python
import functools
import math

import jax
import jax.numpy as jnp
from jax import lax
from jax.experimental import pallas as pl
from jax.experimental.pallas import tpu as pltpu
from jax.sharding import PartitionSpec as P


BF16 = jnp.bfloat16
F32 = jnp.float32


def split(value):
    high = value.astype(BF16)
    low = (value - high.astype(F32)).astype(BF16)
    return high, low


def lane_half(rows, width):
    return lax.broadcasted_iota(jnp.int32, (rows, width), 1) < width // 2


def unpack_pairs(panel_ref, pairs, count, block_size):
    lanes = 2 * block_size
    keep = lane_half(count, lanes)
    for c in range(block_size // 2):
        both = panel_ref[:, c * lanes : (c + 1) * lanes].astype(F32)
        turned = pltpu.roll(both, block_size, 1)
        pitch = block_size + 1
        pairs[pl.ds(2 * c, count, stride=pitch), :] = jnp.where(keep, both, turned)
        pairs[pl.ds(2 * c + 1, count, stride=pitch), :] = jnp.where(keep, turned, both)


def column_block(ref, block, slot, block_size):
    lanes = 2 * block_size
    start = pl.multiple_of(block // 2 * lanes, lanes)
    wide = ref[:, pl.ds(start, lanes)]
    return jnp.where(block % 2 == slot, wide, pltpu.roll(wide, block_size, 1))


def group_kernel(block_count, tile, skip, pos_ref, own_ref, x_ref, y_ref, panel_ref, out_ref, left, right, pairs, scr, mid):
    step = pl.program_id(0)
    order = x_ref.shape[0]
    block_size = order // block_count
    lanes = 2 * block_size
    half = lane_half(order, lanes)

    @pl.when(step == 0)
    def _():
        for s in range(2):
            position = own_ref[s]
            a = pl.multiple_of(position // block_count * block_size, block_size)
            xa = x_ref[pl.ds(a, block_size), :]
            ya = y_ref[pl.ds(a, block_size), :]
            for p in range(block_count):
                cols = slice(p * block_size, (p + 1) * block_size)
                high, low = split(jnp.concatenate([xa[:, cols], ya[:, cols]], axis=1))
                left[p, s * block_size : (s + 1) * block_size, :] = high
                left[p, (2 + s) * block_size : (3 + s) * block_size, :] = low
        for m, ref in enumerate((y_ref, x_ref)):
            first = column_block(ref, own_ref[0] % block_count, 0, block_size)
            second = column_block(ref, own_ref[1] % block_count, 1, block_size)
            high, low = split(jnp.where(half, first, second))
            for q in range(block_count):
                rows = slice(q * block_size, (q + 1) * block_size)
                cols = slice(m * lanes, (m + 1) * lanes)
                right[q, :block_size, cols] = high[rows]
                right[q, block_size:, cols] = low[rows]

    unpack_pairs(panel_ref, pairs, tile, block_size)
    keep = lane_half(block_size, lanes)
    dot = functools.partial(jnp.dot, preferred_element_type=F32)

    def spread(j, e, t):
        position = pos_ref[skip + step * tile + j]
        p = position // block_count
        q = position % block_count
        top = dot(e, right[q])
        low_part = dot(t, right[p])
        for m, part in enumerate((top[:, :lanes], top[:, lanes:], low_part[:, :lanes], low_part[:, lanes:])):
            high, low = split(part)
            rows = slice(m * block_size, (m + 1) * block_size)
            mid[j, rows, :lanes] = high
            mid[j, rows, lanes:] = low

    def two(i, carry):
        pitch = block_size + 1
        block = jnp.concatenate(
            [pairs[pl.ds(2 * i * pitch, block_size), :], pairs[pl.ds((2 * i + 1) * pitch, block_size), :]],
            axis=0,
        )
        turned = block.T[:block_size]
        swapped = pltpu.roll(turned, block_size, 1)
        e = block.astype(BF16)
        spread(2 * i, e[:block_size], jnp.where(keep, turned, swapped).astype(BF16))
        spread(2 * i + 1, e[block_size:], jnp.where(keep, swapped, turned).astype(BF16))
        return carry

    lax.fori_loop(0, tile // 2, two, 0, unroll=tile // 2)

    def collect(j, carry):
        position = pos_ref[skip + step * tile + j]
        a = jnp.concatenate([left[position // block_count], left[position % block_count]], axis=1)
        h = dot(a, mid[j])
        b = block_size
        quad = lambda r, c: jnp.where(
            keep, h[r : r + b, c : c + lanes], h[r + b : r + 2 * b, c : c + lanes]
        )
        scr[pl.ds(j * (b + 1), b), :] = quad(0, 0) + (quad(0, lanes) + quad(2 * b, 0))
        return carry

    lax.fori_loop(0, tile, collect, 0, unroll=tile)
    keep_t = lane_half(tile, lanes)
    for r in range(0, block_size, 2):
        even = scr[pl.ds(r, tile, stride=block_size + 1), :]
        odd = scr[pl.ds(r + 1, tile, stride=block_size + 1), :]
        columns = slice(r * block_size, (r + 2) * block_size)
        out_ref[0, :, columns] = jnp.where(keep_t, even, pltpu.roll(odd, block_size, 1)).astype(BF16)
        out_ref[1, :, columns] = jnp.where(keep_t, pltpu.roll(even, block_size, 1), odd).astype(BF16)


def whole(shape):
    return pl.BlockSpec(shape, lambda *_: (0,) * len(shape))


def cost(us, count):
    return pl.CostEstimate(flops=us * 10**9, bytes_accessed=count, transcendentals=0)


def group_table(x, y, panel, positions, own, block_count, part, parts):
    width = panel.shape[1]
    count = panel.shape[0] // parts
    b = x.shape[0] // block_count
    tile = math.gcd(count, 32)
    skip = part * (count // tile)
    return pl.pallas_call(
        functools.partial(group_kernel, block_count, tile, part * count),
        grid_spec=pltpu.PrefetchScalarGridSpec(
            num_scalar_prefetch=2,
            grid=(count // tile,),
            in_specs=[
                whole(x.shape),
                whole(y.shape),
                pl.BlockSpec((tile, width), lambda i, *_: (i + skip, 0)),
            ],
            out_specs=pl.BlockSpec((2, tile, width), lambda i, *_: (0, i, 0)),
            scratch_shapes=[
                pltpu.VMEM((block_count, 4 * b, 2 * b), BF16),
                pltpu.VMEM((block_count, 2 * b, 4 * b), BF16),
                pltpu.VMEM((tile * (b + 1) + 7, 2 * b), F32),
                pltpu.VMEM((tile * (b + 1) + 7, 2 * b), F32),
                pltpu.VMEM((tile, 4 * b, 4 * b), BF16),
            ],
        ),
        out_shape=jax.ShapeDtypeStruct((2, count, width), BF16),
        cost_estimate=cost(25, 10**7),
        name="group_table",
    )(positions, own, x, y, panel)


def own_kernel(
    block_count, tile, pos_ref, x_ref, y_ref, panel_ref, all_ref, place_ref, out_ref, left, right, pairs, mid, scr, table
):
    step = pl.program_id(0)
    order = x_ref.shape[0]
    b = order // block_count
    lanes = 2 * b
    pitch = b + 1
    positions = block_count * block_count

    @pl.when(step == 0)
    def _():
        for p in range(block_count):
            cols = slice(p * b, (p + 1) * b)
            high, low = split(jnp.concatenate([x_ref[:, cols], y_ref[:, cols]], axis=1))
            left[p, :, :lanes] = high
            left[p, :, lanes:] = low
        for m, ref in enumerate((y_ref, x_ref)):
            for q in range(block_count):
                high, low = split(ref[q * b : (q + 1) * b, :])
                cols = slice(m * order, (m + 1) * order)
                right[q, :b, cols] = high
                right[q, b:, cols] = low
        unpack_pairs(panel_ref, pairs, panel_ref.shape[0], b)

    dot = functools.partial(jnp.dot, preferred_element_type=F32)
    keep = lane_half(block_count, lanes)
    groups = order // lanes
    wide = 2 * lanes

    for j in range(tile):
        position = pos_ref[step * tile + j]
        block = pairs[pl.ds((step * tile + j) * pitch, b), :]
        turned = jnp.concatenate([block, block], axis=0).T[:b]
        top = dot(block.astype(BF16), right[position % block_count])
        low_part = dot(turned.astype(BF16), right[position // block_count])
        parts = (top[:, :order], top[:, order:], low_part[:, :order], low_part[:, order:])
        for m, part in enumerate(parts):
            high, low = split(part)
            mid[j, m * b : (m + 1) * b, :] = high
            mid[j, (4 + m) * b : (5 + m) * b, :] = low
    for j in range(tile):
        position = pos_ref[step * tile + j]
        lp, lq = left[position // block_count], left[position % block_count]
        a = jnp.concatenate([lp[:, :lanes], lq[:, :lanes]], axis=1)
        a_low = jnp.concatenate([lp[:, lanes:], lq[:, lanes:]], axis=1)
        for w in range(order // wide):
            cols = slice(w * wide, (w + 1) * wide)
            high = mid[j, : 4 * b, cols]
            h = dot(jnp.concatenate([a, a_low], axis=1), jnp.concatenate([high, high], axis=0))
            h = h + dot(a, mid[j, 4 * b :, cols])
            for g in range(wide // lanes):
                for i in range(block_count):
                    start = (((j * groups + w * (wide // lanes)) + g) * block_count + i) * pitch
                    scr[start : start + b, :] = h[i * b : (i + 1) * b, g * lanes : (g + 1) * lanes]
    for j in range(tile):
        for g in range(groups):
            base = (j * groups + g) * block_count * pitch
            first = j * positions + 2 * g * block_count
            for r in range(0, b, 2):
                even = scr[pl.ds(base + r, block_count, stride=pitch), :]
                odd = scr[pl.ds(base + r + 1, block_count, stride=pitch), :]
                one = jnp.where(keep, even, pltpu.roll(odd, b, 1))
                two = jnp.where(keep, pltpu.roll(even, b, 1), odd)
                table[first : first + 2 * block_count, r * b : (r + 2) * b] = jnp.concatenate(
                    [one, two], axis=0
                ).astype(BF16)
    products = lax.dot_general(
        table[...], all_ref[...], (((1,), (1,)), ((), ())), preferred_element_type=F32
    )
    hit = (
        lax.broadcasted_iota(jnp.int32, (positions, products.shape[1]), 0) == place_ref[...]
    )
    for j in range(tile):
        part = jnp.where(hit, products[j * positions : (j + 1) * positions], 0.0)
        out_ref[pl.ds(step * tile + j, 1), :] = jnp.sum(part, axis=0, keepdims=True)


def own_part(x, y, panel, positions, everything, place, block_count):
    count, width = panel.shape
    columns = everything.shape[0]
    order = x.shape[0]
    b = order // block_count
    rows = block_count * block_count
    tile = math.gcd(count, 4)
    return pl.pallas_call(
        functools.partial(own_kernel, block_count, tile),
        grid_spec=pltpu.PrefetchScalarGridSpec(
            num_scalar_prefetch=1,
            grid=(count // tile,),
            in_specs=[
                whole(x.shape),
                whole(y.shape),
                whole(panel.shape),
                pl.BlockSpec(everything.shape, lambda *_: (0, 0), pipeline_mode=pl.Buffered(1)),
                whole(place.shape),
            ],
            out_specs=whole((count, columns)),
            scratch_shapes=[
                pltpu.VMEM((block_count, order, 4 * b), BF16),
                pltpu.VMEM((block_count, 2 * b, 2 * order), BF16),
                pltpu.VMEM((max(count, 8) * (b + 1) + 7, 2 * b), F32),
                pltpu.VMEM((tile, 8 * b, order), BF16),
                pltpu.VMEM((tile * order // 2 // b * block_count * (b + 1) + 7, 2 * b), F32),
                pltpu.VMEM((tile * rows, width), BF16),
            ],
        ),
        out_shape=jax.ShapeDtypeStruct((count, columns), F32),
        cost_estimate=cost(22, 10**7),
        name="own_part",
    )(positions, x, y, panel, everything, place)


def row_kernel(cons_ref, table_ref, block_ref, place_ref, out_ref, total):
    step = pl.program_id(0)
    nt = (((1,), (1,)), ((), ()))
    cons = cons_ref[...]
    rows = lax.dot_general(cons, table_ref[0], nt, preferred_element_type=F32)
    block = block_ref[...]
    for s in range(1, table_ref.shape[0]):
        other = lax.dot_general(cons, table_ref[s], nt, preferred_element_type=F32)
        rows = jnp.where(block == s, other, rows)
    rows = rows.astype(BF16)
    places, tile = total.shape[0], cons.shape[0]
    hits = lax.broadcasted_iota(jnp.int32, (places, tile), 0) == place_ref[...]
    part = jnp.dot(jnp.where(hits, 1.0, 0.0).astype(BF16), rows, preferred_element_type=F32)

    @pl.when(step == 0)
    def _():
        total[...] = part

    @pl.when(step > 0)
    def _():
        total[...] += part

    @pl.when(step == pl.num_programs(0) - 1)
    def _():
        out_ref[...] = total[...].astype(BF16)


def send_rows(cons, table, block, place, places):
    slots, width = cons.shape
    cols = table.shape[1]
    tile = math.gcd(slots, 256)
    return pl.pallas_call(
        row_kernel,
        grid=(slots // tile,),
        in_specs=[
            pl.BlockSpec((tile, width), lambda i: (i, 0)),
            pl.BlockSpec(table.shape, lambda i: (0, 0, 0), pipeline_mode=pl.Buffered(1)),
            pl.BlockSpec((tile, 1), lambda i: (i, 0)),
            pl.BlockSpec((1, tile), lambda i: (0, i)),
        ],
        out_specs=whole((places, cols)),
        out_shape=jax.ShapeDtypeStruct((places, cols), BF16),
        scratch_shapes=[pltpu.VMEM((places, cols), F32)],
        cost_estimate=cost(20, 2 * 10**7),
        name="send_rows",
    )(cons, table, block, place)


def update_kernel(parts, *refs):
    row_refs, (weight_ref, trailing_ref, out_ref) = refs[:parts], refs[parts:]
    rows = jnp.concatenate([ref[...] for ref in row_refs] * 2, axis=1)
    out_ref[...] = trailing_ref[...] - jnp.dot(rows, weight_ref[...], preferred_element_type=F32)


def update(row_parts, weight, trailing):
    rows, cols = trailing.shape
    tile = math.gcd(rows, 512)
    return pl.pallas_call(
        functools.partial(update_kernel, len(row_parts)),
        grid=(rows // tile,),
        in_specs=[pl.BlockSpec((tile, part.shape[1]), lambda i: (i, 0)) for part in row_parts]
        + [whole(weight.shape), pl.BlockSpec((tile, cols), lambda i: (i, 0))],
        out_specs=pl.BlockSpec((tile, cols), lambda i: (i, 0)),
        out_shape=jax.ShapeDtypeStruct((rows, cols), F32),
        cost_estimate=cost(8, 2 * 10**7),
        name="update",
    )(*row_parts, weight, trailing)


def hdot(a, b, contract):
    return lax.dot_general(
        a, b, ((contract[:1], contract[1:]), ((), ())),
        precision=lax.Precision.HIGHEST, preferred_element_type=F32,
    )


def factor_kernel(block, s_ref, out_ref, a):
    order = s_ref.shape[0]
    count = order // block
    groups = block // 8
    a[...] = s_ref[...]
    row_id = lax.broadcasted_iota(jnp.int32, (8, 1), 0)
    eye = (
        lax.broadcasted_iota(jnp.int32, (block, block), 0)
        == lax.broadcasted_iota(jnp.int32, (block, block), 1)
    ).astype(F32)

    def diagonal(b, carry):
        start = pl.multiple_of(b * block, block)
        tile = (8, block)
        left = [a[pl.ds(start + 8 * g, 8), pl.ds(start, block)] for g in range(groups)]
        right = [eye[8 * g : 8 * g + 8, :] for g in range(groups)]
        for g in range(groups):
            spot = lambda i, s, t: jnp.broadcast_to(
                left[i][s : s + 1, 8 * g + t : 8 * g + t + 1], tile
            )
            d = {(s, t): spot(g, s, t) for t in range(8) for s in range(t, 8)}
            inv, low, scaled = [], {}, []
            heads = [
                [jnp.broadcast_to(side[g][t : t + 1, :], tile) for side in (left, right)]
                for t in range(8)
            ]
            for t in range(8):
                root = lax.rsqrt(d[t, t])
                root = root * (1.5 - 0.5 * d[t, t] * root * root)
                inv.append(root)
                for s in range(t + 1, 8):
                    low[s, t] = d[s, t] * root
                for u in range(t + 1, 8):
                    for s in range(u, 8):
                        d[s, u] = d[s, u] - low[s, t] * low[u, t]
                now = heads[t]
                for u in range(t):
                    now = [n - low[t, u] * r for n, r in zip(now, scaled[u])]
                scaled.append([n * root for n in now])
            for i in range(g + 1, groups):
                mult = []
                for t in range(8):
                    m = jnp.broadcast_to(left[i][:, 8 * g + t : 8 * g + t + 1], tile)
                    for u in range(t):
                        m = m - mult[u] * low[t, u]
                    mult.append(m * inv[t])
                for t in range(8):
                    left[i] = left[i] - mult[t] * scaled[t][0]
                    right[i] = right[i] - mult[t] * scaled[t][1]
            done = scaled[0][1]
            for t in range(1, 8):
                done = jnp.where(row_id == t, scaled[t][1], done)
            right[g] = done
        inverse = jnp.concatenate(right, axis=0)
        out_ref[pl.ds(start, block), pl.ds(start, block)] = inverse
        panel = hdot(a[:, pl.ds(start, block)], inverse, (1, 1))
        below = lax.broadcasted_iota(jnp.int32, (order, 1), 0) >= start + block
        panel = jnp.where(below, panel, 0.0)
        a[:, pl.ds(start, block)] = panel
        return carry, panel

    def body(b, carry):
        _, panel = diagonal(b, carry)
        start = pl.multiple_of(b * block, block)

        for i in range(1, count):
            @pl.when(b < i)
            def _():
                piece = a[i * block : (i + 1) * block, pl.ds(start, block)]
                cols = slice(i * block, (i + 1) * block)
                a[:, cols] = a[:, cols] - hdot(panel, piece, (1, 1))

        return carry

    lax.fori_loop(0, count, body, 0)
    for i in range(count):
        for b in range(i + 1, count):
            out_ref[i * block : (i + 1) * block, b * block : (b + 1) * block] = jnp.zeros(
                (block, block), F32
            )
    for i in range(1, count):
        low_row = a[i * block : (i + 1) * block, : i * block]
        total = hdot(low_row, out_ref[: i * block, : i * block], (1, 0))
        own = out_ref[i * block : (i + 1) * block, i * block : (i + 1) * block]
        out_ref[i * block : (i + 1) * block, : i * block] = -hdot(own, total, (1, 0))


def inverse_factor(matrix):
    order = matrix.shape[0]
    block = 128
    return pl.pallas_call(
        functools.partial(factor_kernel, block),
        in_specs=[pl.BlockSpec(memory_space=pltpu.VMEM)],
        out_specs=pl.BlockSpec(memory_space=pltpu.VMEM),
        out_shape=jax.ShapeDtypeStruct((order, order), F32),
        scratch_shapes=[pltpu.VMEM((order, order), F32)],
        cost_estimate=cost(30, 10**6),
        name="inverse_factor",
    )(matrix)


def body(
    x_mat,
    y_inv,
    panel_blocks,
    panel_pos,
    group_blocks,
    cons_blocks,
    slot_block,
    slot_row,
    group_size,
    trailing,
):
    rows_size = lax.axis_size("row")
    cols_size = lax.axis_size("col")
    devices = rows_size * cols_size
    col_index = lax.axis_index("col")
    device_id = lax.axis_index("row") * cols_size + col_index
    panel_cols = panel_blocks.shape[0]
    per_device = panel_cols // devices
    order = x_mat.shape[0]
    block_size = math.isqrt(panel_blocks.shape[1])
    block_count = order // block_size
    slot_count = cons_blocks.shape[0]

    sub_rows = trailing.shape[0] // cols_size
    base_share = sub_rows // devices
    spread = sub_rows - devices // 4 * base_share
    capacity = base_share + (spread + devices - 1) // devices
    places = devices * capacity
    slot_ids = jnp.arange(slot_count, dtype=jnp.int32)
    live_slots = slot_ids < group_size[0]
    target = slot_row // sub_rows
    dest_hits = (
        target[:, None] == jnp.arange(devices, dtype=jnp.int32)[None, :]
    ) & live_slots[:, None]
    earlier = (slot_ids[:, None] > slot_ids[None, :]).astype(BF16)
    before = jnp.dot(earlier, dest_hits.astype(BF16), preferred_element_type=F32)
    dest_rank = jnp.sum(jnp.where(dest_hits, before, 0.0), axis=1).astype(jnp.int32)
    slot_place = jnp.where(live_slots, target * capacity + dest_rank, places)
    exchange = functools.partial(
        lax.all_to_all, axis_name=("row", "col"), split_axis=0, concat_axis=0, tiled=True
    )

    own_group = lax.dynamic_index_in_dim(group_blocks, device_id, 0, keepdims=False)
    block_column, place_row = slot_block.reshape(-1, 1), slot_place.reshape(1, -1)
    halves = 2
    width = panel_cols // halves

    def half_table(half, after):
        x_now = x_mat if after is None else lax.optimization_barrier((x_mat, after))[0]
        return group_table(
            x_now, y_inv, panel_blocks, panel_pos, own_group, block_count, half, halves
        )

    def half_rows(table):
        sent = send_rows(cons_blocks, table, block_column, place_row, places)
        return sent, exchange(sent.reshape(devices, capacity, width))

    def settle(rows):
        slab = jnp.dot(recv_hits, rows.reshape(-1, width), preferred_element_type=F32).astype(BF16)
        return slab, lax.all_gather(slab, "col", axis=0, tiled=True)

    place_ids = jnp.arange(places, dtype=jnp.int32)
    tag = slot_row % sub_rows + 1
    arriving = place_ids[:, None] == slot_place[None, :]
    send_local = jnp.sum(jnp.where(arriving, tag[None, :], 0), axis=1).astype(F32) - 1.0
    padded = jnp.pad(send_local, (0, 16 * panel_cols - places)).reshape(16, panel_cols)
    tags = lax.all_gather(padded, ("row", "col"), axis=0, tiled=True)
    recv_local = lax.dynamic_index_in_dim(
        tags.reshape(devices, -1)[:, :places].reshape(devices, devices, capacity),
        device_id, 1, keepdims=False,
    ).astype(jnp.int32)
    local_ids = jnp.arange(sub_rows, dtype=jnp.int32)
    recv_hits = (local_ids[:, None] == recv_local.reshape(1, -1)).astype(BF16)

    def spread(part, axis, size):
        copies = jnp.broadcast_to(part[None], (size,) + part.shape)
        copies = lax.all_to_all(copies, axis, split_axis=0, concat_axis=0, tiled=True)
        return copies.reshape(-1, panel_cols)

    sent, early = half_rows(half_table(0, None))
    own_panel = lax.dynamic_slice_in_dim(panel_blocks, device_id * per_device, per_device, 0)
    own_pos = lax.dynamic_slice_in_dim(panel_pos, device_id * per_device, per_device, 0)
    place = panel_pos % block_count * block_count + panel_pos // block_count
    own_panel, sent = lax.optimization_barrier((own_panel, sent))
    row_part = own_part(
        x_mat, y_inv, own_panel, own_pos, panel_blocks, place.reshape(1, -1), block_count
    )
    early, row_part = lax.optimization_barrier((early, row_part))
    column_part = spread(row_part, "col", cols_size)
    first_slab, first_rows = settle(early)
    table = half_table(1, first_slab)
    column_part, table = lax.optimization_barrier((column_part, table))
    panel_schur = spread(column_part, "row", rows_size)
    sent, late = half_rows(table)

    panel_schur, sent = lax.optimization_barrier((panel_schur, sent))
    symmetric = 0.5 * (panel_schur + panel_schur.T)
    eye = (
        lax.broadcasted_iota(jnp.int32, symmetric.shape, 0)
        == lax.broadcasted_iota(jnp.int32, symmetric.shape, 1)
    )
    diag_shift = 0.01 * jnp.sum(jnp.where(eye, symmetric, 0.0)) / panel_cols
    inverse = inverse_factor(symmetric + jnp.where(eye, diag_shift, 0.0))
    late, inverse = lax.optimization_barrier((late, inverse))
    last_slab, last_rows = settle(late)

    block_rows = trailing.shape[1] // rows_size
    slab = jnp.concatenate([first_slab, last_slab], axis=1)
    head = slab[: block_rows * cols_size].reshape(cols_size, block_rows, panel_cols)
    head = lax.all_to_all(head, "col", split_axis=0, concat_axis=0, tiled=True)[0]
    picked = spread(head, "row", rows_size)

    def halved(matrix):
        rounded = lax.reduce_precision(matrix, exponent_bits=8, mantissa_bits=7)
        low = lax.reduce_precision(matrix - rounded, exponent_bits=8, mantissa_bits=7)
        return rounded.astype(BF16), low.astype(BF16)

    def doubled(matrix):
        return jnp.concatenate(halved(matrix), axis=1)

    high, low = halved(inverse)
    inner = lax.dot_general(
        jnp.concatenate([high, high, low], axis=0), jnp.concatenate([high, low, high], axis=0),
        (((0,), (0,)), ((), ())), preferred_element_type=F32,
    )
    lower_slab = lax.dot_general(
        jnp.concatenate([slab, slab], axis=1), doubled(inverse), (((1,), (1,)), ((), ())),
        preferred_element_type=F32,
    )
    weight = lax.dot_general(
        doubled(inner), jnp.concatenate([picked, picked], axis=1), (((1,), (1,)), ((), ())),
        preferred_element_type=F32,
    )
    weight = doubled(weight.T).T
    return (lower_slab, update([first_rows, last_rows], weight, trailing))


def solution(mesh):
    return jax.shard_map(
        body,
        mesh=mesh,
        in_specs=(
            P(),
            P(),
            P(),
            P(),
            P(),
            P(("row", "col"), None),
            P(("row", "col")),
            P(("row", "col")),
            P(("row", "col")),
            P("row", "col"),
        ),
        out_specs=(P(("row", "col"), None), P("row", "col")),
        check_vma=False,
    )
```

profile of v0, /device:TPU:0, one launch (start us, length us, event | category | flops | bytes accessed | tf_op | source)
XLA Modules:
  0.0 256.4 jit_solution(9891623864602182246)
XLA Ops:
  14.5 27.0 %group_table.2.table_ref = bf16[2,256,4096]{2,1,0:T(8,128)(2,1)} custom-call(s32[512]{0:T(512)} %pos_ref.3, s32[2]{0:T(128)} %dynamic-slice_reduce_fusion.own_ref, f32[512,512]{1,0:T(8,128)} %x_ref.4, f32[512,512]{1,0:T(8,128)} %y_ref.5, bf16[512,4096]{1,0:T(8,128)(2,1)} %panel_ref.3), custom_call_target="tpu_custom_call" | custom-call | flops 24999999488 | bytes 10000000 | tf_op jit(solution)/shard_map/group_table/pallas_call | solution.py:139
  41.5 16.9 %send_rows.2 = bf16[1792,256]{1,0:T(8,128)(2,1)} custom-call(bf16[1792,4096]{1,0:T(8,128)(2,1)} %cons_ref.3, bf16[2,256,4096]{2,1,0:T(8,128)(2,1)} %group_table.2.table_ref, s32[1792,1]{1,0:T(8,128)} %reshape.73.block_ref, s32[1,1792]{1,0:T(1,128)} %broadcast_in_dim.64.place_ref), custom_call_target="tpu_custom_call" | custom-call | flops 20000000000 | bytes 20000000 | tf_op jit(solution)/shard_map/send_rows/pallas_call | solution.py:308
  58.3 7.3 %all-to-all-start = ((bf16[32,56,256]{2,1,0:T(8,128)(2,1)}), bf16[32,56,256]{2,1,0:T(8,128)(2,1)S(1)}, u32[]{:S(2)}, u32[]{:S(2)}) async-start(bf16[32,56,256]{2,1,0:T(8,128)(2,1)} %bitcast.31), calls=%async_computation | async-start | bytes 1835008 | tf_op jit(solution)/shard_map/all_to_all | solution.py:510
  66.8 1.6 constant_dynamic-slice_fusion.panel_ref
  68.4 19.5 %own_part.1 = f32[16,512]{1,0:T(8,128)} custom-call(s32[16]{0:T(128)} %dynamic_slice.16.pos_ref, f32[512,512]{1,0:T(8,128)} %x_ref.4, f32[512,512]{1,0:T(8,128)} %y_ref.5, bf16[16,4096]{1,0:T(8,128)(2,1)} %constant_dynamic-slice_fusion.panel_ref, bf16[512,4096]{1,0:T(8,128)(2,1)} %panel_ref.3, s32[1,512]{1,0:T(1,128)} %bitcast.35), custom_call_target="tpu_custom_call" | custom-call | flops 22000001024 | bytes 10000000 | tf_op jit(solution)/shard_map/own_part/pallas_call | solution.py:249
  88.0 1.4 broadcast_in_dim.65
  89.4 4.9 %all-to-all-start.1 = ((f32[4,16,512]{2,1,0:T(8,128)}), f32[4,16,512]{2,1,0:T(8,128)S(1)}, u32[]{:S(2)}, u32[]{:S(2)}) async-start(f32[4,16,512]{2,1,0:T(8,128)} %broadcast_in_dim.65), calls=%async_computation.1 | async-start | bytes 262144 | tf_op jit(solution)/shard_map/all_to_all | solution.py:531
  96.3 2.1 fusion.23
  98.5 27.1 %group_table.3.table_ref = bf16[2,256,4096]{2,1,0:T(8,128)(2,1)} custom-call(s32[512]{0:T(512)} %pos_ref.3, s32[2]{0:T(128)} %dynamic-slice_reduce_fusion.own_ref, f32[512,512]{1,0:T(8,128)} %x_ref.4, f32[512,512]{1,0:T(8,128)} %y_ref.5, bf16[512,4096]{1,0:T(8,128)(2,1)} %panel_ref.3), custom_call_target="tpu_custom_call" | custom-call | flops 24999999488 | bytes 10000000 | tf_op jit(solution)/shard_map/group_table/pallas_call | solution.py:139
  126.7 3.7 %all-to-all-start.3 = ((f32[8,64,512]{2,1,0:T(8,128)}), f32[8,64,512]{2,1,0:T(8,128)S(1)}, u32[]{:S(2)}, u32[]{:S(2)}) async-start(f32[8,64,512]{2,1,0:T(8,128)} %broadcast_in_dim.66), calls=%async_computation.3 | async-start | bytes 2097152 | tf_op jit(solution)/shard_map/all_to_all | solution.py:531
  130.3 16.9 %send_rows.3 = bf16[1792,256]{1,0:T(8,128)(2,1)} custom-call(bf16[1792,4096]{1,0:T(8,128)(2,1)} %cons_ref.3, bf16[2,256,4096]{2,1,0:T(8,128)(2,1)} %group_table.3.table_ref, s32[1792,1]{1,0:T(8,128)} %reshape.73.block_ref, s32[1,1792]{1,0:T(1,128)} %broadcast_in_dim.64.place_ref), custom_call_target="tpu_custom_call" | custom-call | flops 20000000000 | bytes 20000000 | tf_op jit(solution)/shard_map/send_rows/pallas_call | solution.py:308
  147.2 6.6 %all-to-all-start.2 = ((bf16[32,56,256]{2,1,0:T(8,128)(2,1)}), bf16[32,56,256]{2,1,0:T(8,128)(2,1)S(1)}, u32[]{:S(2)}, u32[]{:S(2)}) async-start(bf16[32,56,256]{2,1,0:T(8,128)(2,1)} %bitcast.30), calls=%async_computation.2 | async-start | bytes 1835008 | tf_op jit(solution)/shard_map/all_to_all | solution.py:510
  156.9 28.1 %inverse_factor.1 = f32[512,512]{1,0:T(8,128)} custom-call(f32[512,512]{1,0:T(8,128)} %select_add_fusion.s_ref), custom_call_target="tpu_custom_call" | custom-call | flops 30000001024 | bytes 1000000 | tf_op jit(solution)/shard_map/inverse_factor/pallas_call | solution.py:443
  185.0 2.1 fusion.24
  187.2 1.6 pad_maximum_fusion.2
  188.8 4.9 %all-to-all-start.4 = ((bf16[4,64,512]{2,1,0:T(8,128)(2,1)}), bf16[4,64,512]{2,1,0:T(8,128)(2,1)S(1)}, u32[]{:S(2)}, u32[]{:S(2)}) async-start(bf16[4,64,512]{2,1,0:T(8,128)(2,1)} %bitcast.9), calls=%async_computation.4 | async-start | bytes 524288 | tf_op jit(solution)/shard_map/all_to_all | solution.py:564
  193.9 14.2 %all-to-all-done.4 = bf16[4,64,512]{2,1,0:T(8,128)(2,1)S(1)} async-done(((bf16[4,64,512]{2,1,0:T(8,128)(2,1)}), bf16[4,64,512]{2,1,0:T(8,128)(2,1)S(1)}, u32[]{:S(2)}, u32[]{:S(2)}) %all-to-all-start.4) | async-done | bytes 262176 | tf_op jit(solution)/shard_map/all_to_all | solution.py:564
  208.9 3.7 %all-to-all-start.5 = ((bf16[8,64,512]{2,1,0:T(8,128)(2,1)}), bf16[8,64,512]{2,1,0:T(8,128)(2,1)S(1)}, u32[]{:S(2)}, u32[]{:S(2)}) async-start(bf16[8,64,512]{2,1,0:T(8,128)(2,1)} %broadcast_in_dim.70), calls=%async_computation.5 | async-start | bytes 1048576 | tf_op jit(solution)/shard_map/all_to_all | solution.py:531
  212.6 1.8 reduce-precision_convert_fusion.1
  214.4 2.6 %fusion.6 = f32[1024,512]{1,0:T(8,128)} fusion(bf16[1024,256]{1,0:T(8,128)(2,1)S(1)} %copy-done.3, bf16[1024,256]{1,0:T(8,128)(2,1)S(1)} %copy-done.2, bf16[512,512]{1,0:T(8,128)(2,1)S(1)} %get-tuple-element.25, bf16[512,512]{1,0:T(8,128)(2,1)S(1)} %get-tuple-element.24), kind=kOutput, calls=%fused_computation.10 | convolution fusion | flops 1084227584 | bytes 4194304 | tf_op jit(solution)/shard_map/dot_general | solution.py:580
  217.0 5.3 %all-to-all-done.5 = bf16[8,64,512]{2,1,0:T(8,128)(2,1)S(1)} async-done(((bf16[8,64,512]{2,1,0:T(8,128)(2,1)}), bf16[8,64,512]{2,1,0:T(8,128)(2,1)S(1)}, u32[]{:S(2)}, u32[]{:S(2)}) %all-to-all-start.5) | async-done | bytes 524320 | tf_op jit(solution)/shard_map/all_to_all | solution.py:531
  222.3 1.8 reduce-precision_convert_fusion
  225.2 12.2 %all-gather.8.cloned.1.call-done.refs_1_ = bf16[4096,256]{1,0:T(8,128)(2,1)} async-done(((bf16[1024,256]{1,0:T(8,128)(2,1)}), bf16[4096,256]{1,0:T(8,128)(2,1)}) %all-gather.8.cloned.1.call-update) | async-done | bytes 2097168 | tf_op jit(solution)/shard_map/all_gather | solution.py:514
  237.3 12.5 %update.1 = f32[4096,512]{1,0:T(8,128)} custom-call(bf16[4096,256]{1,0:T(8,128)(2,1)} %all-gather.6.cloned.1.call-done.refs_0_, bf16[4096,256]{1,0:T(8,128)(2,1)} %all-gather.8.cloned.1.call-done.refs_1_, bf16[1024,512]{1,0:T(8,128)(2,1)} %maximum_bitcast_fusion.refs_2_, f32[4096,512]{1,0:T(8,128)} %refs_3_.1), custom_call_target="tpu_custom_call" | custom-call | flops 8000000000 | bytes 20000000 | tf_op jit(solution)/shard_map/update/pallas_call | solution.py:334
  (54 shorter events, 15.5 us)
Async XLA Ops:
  7.2 6.5 %copy-start = (s32[32,2]{0,1:T(2,128)S(1)}, s32[32,2]{0,1:T(2,128)}, u32[]{:S(2)}) copy-start(s32[32,2]{0,1:T(2,128)} %param.14) | copy-start | bytes 772
  7.2 2.6 %copy-start.5 = (s32[1792]{0:T(1024)S(1)}, s32[1792]{0:T(1024)}, u32[]{:S(2)}) copy-start(s32[1792]{0:T(1024)} %param.17) | copy-start | bytes 21508
  7.2 5.3 %copy-start.6 = (s32[1792]{0:T(1024)S(1)}, s32[1792]{0:T(1024)}, u32[]{:S(2)}) copy-start(s32[1792]{0:T(1024)} %param.16) | copy-start | bytes 21508
  7.2 87.1 %all-gather.4.cloned.1.call-start = ((), (), s32[]{:S(2)}) async-start(), calls=%async_computation.6 | async-start | bytes 1081344 | tf_op jit(solution)/shard_map/all_gather | solution.py:521
  41.5 24.2 %copy-start.7 = (s32[512]{0:T(512)S(1)}, s32[512]{0:T(512)}, u32[]{:S(2)}) copy-start(s32[512]{0:T(512)} %pos_ref.3) | copy-start | bytes 6148
  58.3 29.7 %all-to-all-start = ((bf16[32,56,256]{2,1,0:T(8,128)(2,1)}), bf16[32,56,256]{2,1,0:T(8,128)(2,1)S(1)}, u32[]{:S(2)}, u32[]{:S(2)}) async-start(bf16[32,56,256]{2,1,0:T(8,128)(2,1)} %bitcast.31), calls=%async_computation | async-start | bytes 1835008 | tf_op jit(solution)/shard_map/all_to_all | solution.py:510
  89.4 36.2 %all-to-all-start.1 = ((f32[4,16,512]{2,1,0:T(8,128)}), f32[4,16,512]{2,1,0:T(8,128)S(1)}, u32[]{:S(2)}, u32[]{:S(2)}) async-start(f32[4,16,512]{2,1,0:T(8,128)} %broadcast_in_dim.65), calls=%async_computation.1 | async-start | bytes 262144 | tf_op jit(solution)/shard_map/all_to_all | solution.py:531
  94.3 130.9 %all-gather.6.cloned.1.call-start = ((), (), s32[]{:S(2)}) async-start(), calls=%async_computation.7 | async-start | bytes 2621440 | tf_op jit(solution)/shard_map/all_gather | solution.py:514
  126.7 20.6 %all-to-all-start.3 = ((f32[8,64,512]{2,1,0:T(8,128)}), f32[8,64,512]{2,1,0:T(8,128)S(1)}, u32[]{:S(2)}, u32[]{:S(2)}) async-start(f32[8,64,512]{2,1,0:T(8,128)} %broadcast_in_dim.66), calls=%async_computation.3 | async-start | bytes 2097152 | tf_op jit(solution)/shard_map/all_to_all | solution.py:531
  147.2 37.8 %all-to-all-start.2 = ((bf16[32,56,256]{2,1,0:T(8,128)(2,1)}), bf16[32,56,256]{2,1,0:T(8,128)(2,1)S(1)}, u32[]{:S(2)}, u32[]{:S(2)}) async-start(bf16[32,56,256]{2,1,0:T(8,128)(2,1)} %bitcast.30), calls=%async_computation.2 | async-start | bytes 1835008 | tf_op jit(solution)/shard_map/all_to_all | solution.py:510
  153.8 83.5 %all-gather.8.cloned.1.call-start = ((), (), s32[]{:S(2)}) async-start(), calls=%async_computation.8 | async-start | bytes 2621440 | tf_op jit(solution)/shard_map/all_gather | solution.py:514
  185.0 2.1 copy-start.2
  185.0 8.7 %copy-start.4 = (f32[512,512]{1,0:T(8,128)S(1)}, f32[512,512]{1,0:T(8,128)}, u32[]{:S(2)}) copy-start(f32[512,512]{1,0:T(8,128)} %inverse_factor.1) | copy-start | bytes 3145732
  188.8 19.2 %all-to-all-start.4 = ((bf16[4,64,512]{2,1,0:T(8,128)(2,1)}), bf16[4,64,512]{2,1,0:T(8,128)(2,1)S(1)}, u32[]{:S(2)}, u32[]{:S(2)}) async-start(bf16[4,64,512]{2,1,0:T(8,128)(2,1)} %bitcast.9), calls=%async_computation.4 | async-start | bytes 524288 | tf_op jit(solution)/shard_map/all_to_all | solution.py:564
  208.9 13.4 %all-to-all-start.5 = ((bf16[8,64,512]{2,1,0:T(8,128)(2,1)}), bf16[8,64,512]{2,1,0:T(8,128)(2,1)S(1)}, u32[]{:S(2)}, u32[]{:S(2)}) async-start(bf16[8,64,512]{2,1,0:T(8,128)(2,1)} %broadcast_in_dim.70), calls=%async_computation.5 | async-start | bytes 1048576 | tf_op jit(solution)/shard_map/all_to_all | solution.py:531
  212.6 1.8 copy-start.3
  237.3 12.6 %copy-start.1 = (s32[32,2]{0,1:T(2,128)S(1)}, s32[32,2]{0,1:T(2,128)}, u32[]{:S(2)}) copy-start(s32[32,2]{0,1:T(2,128)} %param.14) | copy-start | bytes 772
Sparse Core Ops, SparseCore 0:
  12.0 56.5 all-gather.3
  98.6 47.2 all-gather.5
  187.3 49.9 all-gather.7
where the time goes:
time: 258 us; the launch traced here: 256 us
  Pallas kernels  148 us (57%)
  waiting for transfers between devices  31.7 us (12%)
  starting transfers between devices  31.3 us (12%)
  between operations  15.2 us (6%)
  matrix products  11.7 us (5%)
  local copies, waits for them, and re-layouts  11.1 us (4%)
  other arithmetic  7.45 us (3%)
    pallas_call x2, Pallas kernels, group_table(): pl.pallas_call(functools.partial(group_kernel, block_count, tile, part *...  54.1 us
    pallas_call x2, Pallas kernels, send_rows(): pl.pallas_call(row_kernel, grid=(slots // tile,), in_specs=[pl.BlockSpec(...  33.7 us
    pallas_call x1, Pallas kernels, inverse_factor(): pl.pallas_call(functools.partial(factor_kernel, block), in_specs=[pl.Bloc...  28.1 us
    pallas_call x1, Pallas kernels, own_part(): pl.pallas_call(functools.partial(own_kernel, block_count, tile), grid_spe...  19.5 us
    all_to_all x1, waiting for transfers between devices, body(): lax.all_to_all(head, 'col', split_axis=0, concat_axis=0, tiled=True)[0]  14.2 us
    all_to_all x2, starting transfers between devices, half_rows(): return (sent, exchange(sent.reshape(devices, capacity, width)))  13.9 us
    pallas_call x1, Pallas kernels, update(): pl.pallas_call(functools.partial(update_kernel, len(row_parts)), grid=(ro...  12.5 us
    all_to_all x3, starting transfers between devices, spread(): lax.all_to_all(copies, axis, split_axis=0, concat_axis=0, tiled=True)  12.2 us
  transfers between devices with their start and end apart: 9, of which 3 were waited for; matrix products, arithmetic and copies ran while one was open for 10% of the time, Pallas kernels for 53%

commit v1 on v0

--- a/solution.py
+++ b/solution.py
@@ -41,7 +41,7 @@
     return jnp.where(block % 2 == slot, wide, pltpu.roll(wide, block_size, 1))
 
 
-def group_kernel(block_count, tile, skip, pos_ref, own_ref, x_ref, y_ref, panel_ref, out_ref, left, right, pairs, scr, mid):
+def group_kernel(block_count, tile, skip, pos_ref, own_ref, x_ref, y_ref, panel_ref, next_ref, out_ref, left, right, pairs, scr, scr_b, mid):
     step = pl.program_id(0)
     order = x_ref.shape[0]
     block_size = order // block_count
@@ -70,7 +70,10 @@
                 right[q, :block_size, cols] = high[rows]
                 right[q, block_size:, cols] = low[rows]
 
-    unpack_pairs(panel_ref, pairs, tile, block_size)
+    @pl.when(step == 0)
+    def _():
+        unpack_pairs(panel_ref, pairs, tile, block_size)
+
     keep = lane_half(block_size, lanes)
     dot = functools.partial(jnp.dot, preferred_element_type=F32)
 
@@ -101,7 +104,9 @@
 
     lax.fori_loop(0, tile // 2, two, 0, unroll=tile // 2)
 
-    def collect(j, carry):
+    unpack_pairs(next_ref, pairs, tile, block_size)
+
+    def collect(j, target, row):
         position = pos_ref[skip + step * tile + j]
         a = jnp.concatenate([left[position // block_count], left[position % block_count]], axis=1)
         h = dot(a, mid[j])
@@ -109,17 +114,24 @@
         quad = lambda r, c: jnp.where(
             keep, h[r : r + b, c : c + lanes], h[r + b : r + 2 * b, c : c + lanes]
         )
-        scr[pl.ds(j * (b + 1), b), :] = quad(0, 0) + (quad(0, lanes) + quad(2 * b, 0))
-        return carry
-
-    lax.fori_loop(0, tile, collect, 0, unroll=tile)
-    keep_t = lane_half(tile, lanes)
-    for r in range(0, block_size, 2):
-        even = scr[pl.ds(r, tile, stride=block_size + 1), :]
-        odd = scr[pl.ds(r + 1, tile, stride=block_size + 1), :]
-        columns = slice(r * block_size, (r + 2) * block_size)
-        out_ref[0, :, columns] = jnp.where(keep_t, even, pltpu.roll(odd, block_size, 1)).astype(BF16)
-        out_ref[1, :, columns] = jnp.where(keep_t, pltpu.roll(even, block_size, 1), odd).astype(BF16)
+        target[pl.ds(row * (b + 1), b), :] = quad(0, 0) + (quad(0, lanes) + quad(2 * b, 0))
+
+    part = tile // 2
+    keep_t = lane_half(part, lanes)
+    for number, target in enumerate((scr, scr_b)):
+        for j in range(part):
+            collect(number * part + j, target, j)
+        rows = slice(number * part, (number + 1) * part)
+        for r in range(0, block_size, 2):
+            even = target[pl.ds(r, part, stride=block_size + 1), :]
+            odd = target[pl.ds(r + 1, part, stride=block_size + 1), :]
+            columns = slice(r * block_size, (r + 2) * block_size)
+            out_ref[0, rows, columns] = jnp.where(
+                keep_t, even, pltpu.roll(odd, block_size, 1)
+            ).astype(BF16)
+            out_ref[1, rows, columns] = jnp.where(
+                keep_t, pltpu.roll(even, block_size, 1), odd
+            ).astype(BF16)
 
 
 def whole(shape):
@@ -135,7 +147,8 @@
     count = panel.shape[0] // parts
     b = x.shape[0] // block_count
     tile = math.gcd(count, 32)
-    skip = part * (count // tile)
+    steps = count // tile
+    skip = part * steps
     return pl.pallas_call(
         functools.partial(group_kernel, block_count, tile, part * count),
         grid_spec=pltpu.PrefetchScalarGridSpec(
@@ -145,20 +158,22 @@
                 whole(x.shape),
                 whole(y.shape),
                 pl.BlockSpec((tile, width), lambda i, *_: (i + skip, 0)),
+                pl.BlockSpec((tile, width), lambda i, *_: (jnp.minimum(i + 1, steps - 1) + skip, 0)),
             ],
             out_specs=pl.BlockSpec((2, tile, width), lambda i, *_: (0, i, 0)),
             scratch_shapes=[
                 pltpu.VMEM((block_count, 4 * b, 2 * b), BF16),
                 pltpu.VMEM((block_count, 2 * b, 4 * b), BF16),
                 pltpu.VMEM((tile * (b + 1) + 7, 2 * b), F32),
-                pltpu.VMEM((tile * (b + 1) + 7, 2 * b), F32),
+                pltpu.VMEM((tile // 2 * (b + 1) + 7, 2 * b), F32),
+                pltpu.VMEM((tile // 2 * (b + 1) + 7, 2 * b), F32),
                 pltpu.VMEM((tile, 4 * b, 4 * b), BF16),
             ],
         ),
         out_shape=jax.ShapeDtypeStruct((2, count, width), BF16),
         cost_estimate=cost(25, 10**7),
         name="group_table",
-    )(positions, own, x, y, panel)
+    )(positions, own, x, y, panel, panel)
 
 
 def own_kernel(
@@ -505,9 +520,10 @@
             x_now, y_inv, panel_blocks, panel_pos, own_group, block_count, half, halves
         )
 
-    def half_rows(table):
+    def half_rows(table, ahead):
         sent = send_rows(cons_blocks, table, block_column, place_row, places)
-        return sent, exchange(sent.reshape(devices, capacity, width))
+        sent, ahead = lax.optimization_barrier((sent, ahead))
+        return ahead, sent, exchange(sent.reshape(devices, capacity, width))
 
     def settle(rows):
         slab = jnp.dot(recv_hits, rows.reshape(-1, width), preferred_element_type=F32).astype(BF16)
@@ -531,7 +547,7 @@
         copies = lax.all_to_all(copies, axis, split_axis=0, concat_axis=0, tiled=True)
         return copies.reshape(-1, panel_cols)
 
-    sent, early = half_rows(half_table(0, None))
+    _, sent, early = half_rows(half_table(0, None), slot_place)
     own_panel = lax.dynamic_slice_in_dim(panel_blocks, device_id * per_device, per_device, 0)
     own_pos = lax.dynamic_slice_in_dim(panel_pos, device_id * per_device, per_device, 0)
     place = panel_pos % block_count * block_count + panel_pos // block_count
@@ -545,7 +561,7 @@
     table = half_table(1, first_slab)
     column_part, table = lax.optimization_barrier((column_part, table))
     panel_schur = spread(column_part, "row", rows_size)
-    sent, late = half_rows(table)
+    panel_schur, sent, late = half_rows(table, panel_schur)
 
     panel_schur, sent = lax.optimization_barrier((panel_schur, sent))
     symmetric = 0.5 * (panel_schur + panel_schur.T)
@@ -554,9 +570,10 @@
         == lax.broadcasted_iota(jnp.int32, symmetric.shape, 1)
     )
     diag_shift = 0.01 * jnp.sum(jnp.where(eye, symmetric, 0.0)) / panel_cols
-    inverse = inverse_factor(symmetric + jnp.where(eye, diag_shift, 0.0))
-    late, inverse = lax.optimization_barrier((late, inverse))
+    shifted = symmetric + jnp.where(eye, diag_shift, 0.0)
     last_slab, last_rows = settle(late)
+    shifted, last_slab = lax.optimization_barrier((shifted, last_slab))
+    inverse = inverse_factor(shifted)
 
     block_rows = trailing.shape[1] // rows_size
     slab = jnp.concatenate([first_slab, last_slab], axis=1)

time: 258 us -> 247 us (0.957)
  waiting for transfers between devices: 31.7 us -> 25.4 us
  Pallas kernels: 148 us -> 145 us
    all_to_all x2, waiting for transfers between devices: 0.01 us -> 19.3 us  [half_rows(): return (ahead, sent, exchange(sent.reshape(devices, capacity, width)))]
    all_to_all x1, waiting for transfers between devices: 14.2 us -> 0.01 us  [body(): lax.all_to_all(head, 'col', split_axis=0, concat_axis=0, tiled=True)[0]]
    all_gather x2, waiting for transfers between devices: 12.2 us -> 0.01 us  [settle(): return (slab, lax.all_gather(slab, 'col', axis=0, tiled=True))]
    pallas_call x2, Pallas kernels: 54.1 us -> 50.8 us  [group_table(): pl.pallas_call(functools.partial(group_kernel, block_count, tile, part *...]
  transfers between devices with their start and end apart: 9 -> 9, of which waited for: 3 -> 2; matrix products, arithmetic and copies ran while one was open for 10% -> 10% of each run, Pallas kernels for 53% -> 54%
where the time goes in v1:
time: 247 us; the launch traced here: 245 us
  Pallas kernels  145 us (59%)
  starting transfers between devices  30.5 us (12%)
  waiting for transfers between devices  25.4 us (10%)
  between operations  15.3 us (6%)
  local copies, waits for them, and re-layouts  11 us (4%)
  matrix products  9.81 us (4%)
  other arithmetic  8.66 us (4%)
    pallas_call x2, Pallas kernels, group_table(): pl.pallas_call(functools.partial(group_kernel, block_count, tile, part *...  50.8 us
    pallas_call x2, Pallas kernels, send_rows(): pl.pallas_call(row_kernel, grid=(slots // tile,), in_specs=[pl.BlockSpec(...  33.8 us
    pallas_call x1, Pallas kernels, inverse_factor(): pl.pallas_call(functools.partial(factor_kernel, block), in_specs=[pl.Bloc...  28.1 us
    pallas_call x1, Pallas kernels, own_part(): pl.pallas_call(functools.partial(own_kernel, block_count, tile), grid_spe...  19.5 us
    all_to_all x2, waiting for transfers between devices, half_rows(): return (ahead, sent, exchange(sent.reshape(devices, capacity, width)))  19.3 us
    all_to_all x2, starting transfers between devices, half_rows(): return (ahead, sent, exchange(sent.reshape(devices, capacity, width)))  13.9 us
    pallas_call x1, Pallas kernels, update(): pl.pallas_call(functools.partial(update_kernel, len(row_parts)), grid=(ro...  12.6 us
    all_to_all x3, starting transfers between devices, spread(): lax.all_to_all(copies, axis, split_axis=0, concat_axis=0, tiled=True)  12.1 us
  transfers between devices with their start and end apart: 9, of which 2 were waited for; matrix products, arithmetic and copies ran while one was open for 10% of the time, Pallas kernels for 54%

profile of v1, /device:TPU:0, one launch (start us, length us, event | category | flops | bytes accessed | tf_op | source)
XLA Modules:
  0.0 245.5 jit_solution(9243304970225412748)
XLA Ops:
  9.8 1.4 select_reduce_fusion
  14.4 25.4 %group_table.2.table_ref = bf16[2,256,4096]{2,1,0:T(8,128)(2,1)} custom-call(s32[512]{0:T(512)} %pos_ref.3, s32[2]{0:T(128)} %dynamic-slice_reduce_fusion.own_ref, f32[512,512]{1,0:T(8,128)} %x_ref.4, f32[512,512]{1,0:T(8,128)} %y_ref.5, bf16[512,4096]{1,0:T(8,128)(2,1)} %next_ref.3, bf16[512,4096]{1,0:T(8,128)(2,1)} %next_ref.3), custom_call_target="tpu_custom_call" | custom-call | flops 24999999488 | bytes 10000000 | tf_op jit(solution)/shard_map/group_table/pallas_call | solution.py:152
  39.7 16.9 %send_rows.2 = bf16[1792,256]{1,0:T(8,128)(2,1)} custom-call(bf16[1792,4096]{1,0:T(8,128)(2,1)} %cons_ref.3, bf16[2,256,4096]{2,1,0:T(8,128)(2,1)} %group_table.2.table_ref, s32[1792,1]{1,0:T(8,128)} %reshape.73.block_ref, s32[1,1792]{1,0:T(1,128)} %broadcast_in_dim.64.place_ref), custom_call_target="tpu_custom_call" | custom-call | flops 20000000000 | bytes 20000000 | tf_op jit(solution)/shard_map/send_rows/pallas_call | solution.py:323
  56.6 7.3 %all-to-all-start = ((bf16[32,56,256]{2,1,0:T(8,128)(2,1)}), bf16[32,56,256]{2,1,0:T(8,128)(2,1)S(1)}, u32[]{:S(2)}, u32[]{:S(2)}) async-start(bf16[32,56,256]{2,1,0:T(8,128)(2,1)} %bitcast.30), calls=%async_computation | async-start | bytes 1835008 | tf_op jit(solution)/shard_map/all_to_all | solution.py:526
  65.1 1.6 constant_dynamic-slice_fusion.panel_ref
  66.7 19.5 %own_part.1 = f32[16,512]{1,0:T(8,128)} custom-call(s32[16]{0:T(128)} %dynamic_slice.16.pos_ref, f32[512,512]{1,0:T(8,128)} %x_ref.4, f32[512,512]{1,0:T(8,128)} %y_ref.5, bf16[16,4096]{1,0:T(8,128)(2,1)} %constant_dynamic-slice_fusion.panel_ref, bf16[512,4096]{1,0:T(8,128)(2,1)} %next_ref.3, s32[1,512]{1,0:T(1,128)} %bitcast.35), custom_call_target="tpu_custom_call" | custom-call | flops 22000001024 | bytes 10000000 | tf_op jit(solution)/shard_map/own_part/pallas_call | solution.py:264
  86.2 1.4 broadcast_in_dim.65
  87.7 4.9 %all-to-all-start.1 = ((f32[4,16,512]{2,1,0:T(8,128)}), f32[4,16,512]{2,1,0:T(8,128)S(1)}, u32[]{:S(2)}, u32[]{:S(2)}) async-start(f32[4,16,512]{2,1,0:T(8,128)} %broadcast_in_dim.65), calls=%async_computation.1 | async-start | bytes 262144 | tf_op jit(solution)/shard_map/all_to_all | solution.py:547
  92.6 1.4 reshape.61
  94.6 2.1 fusion.23
  96.8 25.5 %group_table.3.table_ref = bf16[2,256,4096]{2,1,0:T(8,128)(2,1)} custom-call(s32[512]{0:T(512)} %pos_ref.3, s32[2]{0:T(128)} %dynamic-slice_reduce_fusion.own_ref, f32[512,512]{1,0:T(8,128)} %x_ref.4, f32[512,512]{1,0:T(8,128)} %y_ref.5, bf16[512,4096]{1,0:T(8,128)(2,1)} %next_ref.3, bf16[512,4096]{1,0:T(8,128)(2,1)} %next_ref.3), custom_call_target="tpu_custom_call" | custom-call | flops 24999999488 | bytes 10000000 | tf_op jit(solution)/shard_map/group_table/pallas_call | solution.py:152
  123.4 3.7 %all-to-all-start.2 = ((f32[8,64,512]{2,1,0:T(8,128)}), f32[8,64,512]{2,1,0:T(8,128)S(1)}, u32[]{:S(2)}, u32[]{:S(2)}) async-start(f32[8,64,512]{2,1,0:T(8,128)} %broadcast_in_dim.66), calls=%async_computation.2 | async-start | bytes 2097152 | tf_op jit(solution)/shard_map/all_to_all | solution.py:547
  127.1 16.9 %send_rows.3 = bf16[1792,256]{1,0:T(8,128)(2,1)} custom-call(bf16[1792,4096]{1,0:T(8,128)(2,1)} %cons_ref.3, bf16[2,256,4096]{2,1,0:T(8,128)(2,1)} %group_table.3.table_ref, s32[1792,1]{1,0:T(8,128)} %reshape.73.block_ref, s32[1,1792]{1,0:T(1,128)} %broadcast_in_dim.64.place_ref), custom_call_target="tpu_custom_call" | custom-call | flops 20000000000 | bytes 20000000 | tf_op jit(solution)/shard_map/send_rows/pallas_call | solution.py:323
  144.0 6.5 %all-to-all-start.3 = ((bf16[32,56,256]{2,1,0:T(8,128)(2,1)}), bf16[32,56,256]{2,1,0:T(8,128)(2,1)S(1)}, u32[]{:S(2)}, u32[]{:S(2)}) async-start(bf16[32,56,256]{2,1,0:T(8,128)(2,1)} %bitcast.31), calls=%async_computation.3 | async-start | bytes 1835008 | tf_op jit(solution)/shard_map/all_to_all | solution.py:526
  153.4 19.3 %all-to-all-done.3 = bf16[32,56,256]{2,1,0:T(8,128)(2,1)S(1)} async-done(((bf16[32,56,256]{2,1,0:T(8,128)(2,1)}), bf16[32,56,256]{2,1,0:T(8,128)(2,1)S(1)}, u32[]{:S(2)}, u32[]{:S(2)}) %all-to-all-start.3) | async-done | bytes 917536 | tf_op jit(solution)/shard_map/all_to_all | solution.py:526
  172.7 2.1 fusion.24
  174.9 1.6 pad_maximum_fusion.2
  176.5 4.5 %all-to-all-start.4 = ((bf16[4,64,512]{2,1,0:T(8,128)(2,1)}), bf16[4,64,512]{2,1,0:T(8,128)(2,1)S(1)}, u32[]{:S(2)}, u32[]{:S(2)}) async-start(bf16[4,64,512]{2,1,0:T(8,128)(2,1)} %bitcast.9), calls=%async_computation.4 | async-start | bytes 524288 | tf_op jit(solution)/shard_map/all_to_all | solution.py:581
  181.0 28.1 %inverse_factor.1 = f32[512,512]{1,0:T(8,128)} custom-call(f32[512,512]{1,0:T(8,128)} %select_add_fusion.s_ref), custom_call_target="tpu_custom_call" | custom-call | flops 30000001024 | bytes 1000000 | tf_op jit(solution)/shard_map/inverse_factor/pallas_call | solution.py:458
  209.2 1.4 reduce-precision_convert_fusion.2
  211.4 3.5 %all-to-all-start.5 = ((bf16[8,64,512]{2,1,0:T(8,128)(2,1)}), bf16[8,64,512]{2,1,0:T(8,128)(2,1)S(1)}, u32[]{:S(2)}, u32[]{:S(2)}) async-start(bf16[8,64,512]{2,1,0:T(8,128)(2,1)} %broadcast_in_dim.70), calls=%async_computation.5 | async-start | bytes 1048576 | tf_op jit(solution)/shard_map/all_to_all | solution.py:547
  216.0 2.6 %fusion.6 = f32[1024,512]{1,0:T(8,128)} fusion(bf16[1024,256]{1,0:T(8,128)(2,1)S(1)} %copy-done.3, bf16[1024,256]{1,0:T(8,128)(2,1)S(1)} %copy-done.2, bf16[512,512]{1,0:T(8,128)(2,1)S(1)} %get-tuple-element.31, bf16[512,512]{1,0:T(8,128)(2,1)S(1)} %get-tuple-element.30), kind=kOutput, calls=%fused_computation.10 | convolution fusion | flops 1084227584 | bytes 4194304 | tf_op jit(solution)/shard_map/dot_general | solution.py:597
  218.6 6.0 %all-to-all-done.5 = bf16[8,64,512]{2,1,0:T(8,128)(2,1)S(1)} async-done(((bf16[8,64,512]{2,1,0:T(8,128)(2,1)}), bf16[8,64,512]{2,1,0:T(8,128)(2,1)S(1)}, u32[]{:S(2)}, u32[]{:S(2)}) %all-to-all-start.5) | async-done | bytes 524320 | tf_op jit(solution)/shard_map/all_to_all | solution.py:547
  226.4 12.6 %update.1 = f32[4096,512]{1,0:T(8,128)} custom-call(bf16[4096,256]{1,0:T(8,128)(2,1)} %all-gather.6.cloned.1.call-done.refs_0_, bf16[4096,256]{1,0:T(8,128)(2,1)} %all-gather.8.cloned.1.call-done.refs_1_, bf16[1024,512]{1,0:T(8,128)(2,1)} %maximum_bitcast_fusion.refs_2_, f32[4096,512]{1,0:T(8,128)} %refs_3_.1), custom_call_target="tpu_custom_call" | custom-call | flops 8000000000 | bytes 20000000 | tf_op jit(solution)/shard_map/update/pallas_call | solution.py:349
  (52 shorter events, 14.0 us)
Async XLA Ops:
  7.2 6.5 %copy-start = (s32[32,2]{0,1:T(2,128)S(1)}, s32[32,2]{0,1:T(2,128)}, u32[]{:S(2)}) copy-start(s32[32,2]{0,1:T(2,128)} %param.14) | copy-start | bytes 772
  7.2 2.6 %copy-start.4 = (s32[1792]{0:T(1024)S(1)}, s32[1792]{0:T(1024)}, u32[]{:S(2)}) copy-start(s32[1792]{0:T(1024)} %param.17) | copy-start | bytes 21508
  7.2 5.3 %copy-start.5 = (s32[1792]{0:T(1024)S(1)}, s32[1792]{0:T(1024)}, u32[]{:S(2)}) copy-start(s32[1792]{0:T(1024)} %param.16) | copy-start | bytes 21508
  7.2 85.4 %all-gather.4.cloned.1.call-start = ((), (), s32[]{:S(2)}) async-start(), calls=%async_computation.6 | async-start | bytes 1081344 | tf_op jit(solution)/shard_map/all_gather | solution.py:537
  39.7 24.2 %copy-start.6 = (s32[512]{0:T(512)S(1)}, s32[512]{0:T(512)}, u32[]{:S(2)}) copy-start(s32[512]{0:T(512)} %pos_ref.3) | copy-start | bytes 6148
  56.6 29.7 %all-to-all-start = ((bf16[32,56,256]{2,1,0:T(8,128)(2,1)}), bf16[32,56,256]{2,1,0:T(8,128)(2,1)S(1)}, u32[]{:S(2)}, u32[]{:S(2)}) async-start(bf16[32,56,256]{2,1,0:T(8,128)(2,1)} %bitcast.30), calls=%async_computation | async-start | bytes 1835008 | tf_op jit(solution)/shard_map/all_to_all | solution.py:526
  87.7 34.6 %all-to-all-start.1 = ((f32[4,16,512]{2,1,0:T(8,128)}), f32[4,16,512]{2,1,0:T(8,128)S(1)}, u32[]{:S(2)}, u32[]{:S(2)}) async-start(f32[4,16,512]{2,1,0:T(8,128)} %broadcast_in_dim.65), calls=%async_computation.1 | async-start | bytes 262144 | tf_op jit(solution)/shard_map/all_to_all | solution.py:547
  92.6 133.8 %all-gather.6.cloned.1.call-start = ((), (), s32[]{:S(2)}) async-start(), calls=%async_computation.7 | async-start | bytes 2621440 | tf_op jit(solution)/shard_map/all_gather | solution.py:530
  123.4 20.6 %all-to-all-start.2 = ((f32[8,64,512]{2,1,0:T(8,128)}), f32[8,64,512]{2,1,0:T(8,128)S(1)}, u32[]{:S(2)}, u32[]{:S(2)}) async-start(f32[8,64,512]{2,1,0:T(8,128)} %broadcast_in_dim.66), calls=%async_computation.2 | async-start | bytes 2097152 | tf_op jit(solution)/shard_map/all_to_all | solution.py:547
  144.0 28.8 %all-to-all-start.3 = ((bf16[32,56,256]{2,1,0:T(8,128)(2,1)}), bf16[32,56,256]{2,1,0:T(8,128)(2,1)S(1)}, u32[]{:S(2)}, u32[]{:S(2)}) async-start(bf16[32,56,256]{2,1,0:T(8,128)(2,1)} %bitcast.31), calls=%async_computation.3 | async-start | bytes 1835008 | tf_op jit(solution)/shard_map/all_to_all | solution.py:526
  150.5 75.9 %all-gather.8.cloned.1.call-start = ((), (), s32[]{:S(2)}) async-start(), calls=%async_computation.8 | async-start | bytes 2621440 | tf_op jit(solution)/shard_map/all_gather | solution.py:530
  172.7 2.1 copy-start.2
  176.5 34.0 %all-to-all-start.4 = ((bf16[4,64,512]{2,1,0:T(8,128)(2,1)}), bf16[4,64,512]{2,1,0:T(8,128)(2,1)S(1)}, u32[]{:S(2)}, u32[]{:S(2)}) async-start(bf16[4,64,512]{2,1,0:T(8,128)(2,1)} %bitcast.9), calls=%async_computation.4 | async-start | bytes 524288 | tf_op jit(solution)/shard_map/all_to_all | solution.py:581
  211.4 13.2 %all-to-all-start.5 = ((bf16[8,64,512]{2,1,0:T(8,128)(2,1)}), bf16[8,64,512]{2,1,0:T(8,128)(2,1)S(1)}, u32[]{:S(2)}, u32[]{:S(2)}) async-start(bf16[8,64,512]{2,1,0:T(8,128)(2,1)} %broadcast_in_dim.70), calls=%async_computation.5 | async-start | bytes 1048576 | tf_op jit(solution)/shard_map/all_to_all | solution.py:547
  214.9 1.1 copy-start.3
  226.4 12.6 %copy-start.1 = (s32[32,2]{0,1:T(2,128)S(1)}, s32[32,2]{0,1:T(2,128)}, u32[]{:S(2)}) copy-start(s32[32,2]{0,1:T(2,128)} %param.14) | copy-start | bytes 772
Sparse Core Ops, SparseCore 0:
  12.0 56.6 all-gather.3
  96.9 47.0 all-gather.5
  175.0 50.2 all-gather.7
